TPU v7x, 32 devices: a whole 2x2x4 slice. The times are simulated.
32 devices in a mesh: cache: 8 (over z, x), owner: 4 (over y, core).
Axes of the slice: x: 2, y: 2, z: 4, core: 2. Of those that a mesh axis runs over, the one named last changes fastest.
Arguments:
- cache: bfloat16 [32, 4, 128, 256], P('cache'), may hold values from -2.5 to 2.5
- backing: bfloat16 [32, 32, 128, 256], P('cache', 'owner'), may hold values from -2.5 to 2.5
- resident: int32 [32, 4], P('cache'), may hold values from 0 to 31, as said below
- promote: int32 [32, 2], P('cache'), may hold values from 0 to 31, as said below
- victim: int32 [32, 2], P('cache'), may hold values from 0 to 3, as said below
- lookups: int32 [2, 4096, 32, 8], P(None, 'owner', 'cache'), may hold values from 0 to 511
- route: int32 [2, 4, 1024], P(None, 'owner'), may hold values from 0 to 1023, each once within a row
- dcn_down: bfloat16 [8192, 128], P('cache'), may hold values from -0.0625 to 0.0625
- dcn_up: bfloat16 [128, 8192], P(None, 'cache'), may hold values from -0.5 to 0.5
- dcn_bias: float32 [8192], replicated, may hold values from -5 to 5
- mlp_in: bfloat16 [8192, 1024], P('cache'), may hold values from -0.0625 to 0.0625
- mlp_bias: float32 [1024], replicated, may hold values from -3 to 3
- mlp_out: float32 [1024], replicated, may hold values from -0.1875 to 0.1875
- out_bias: float32 [1], replicated, may hold values from -4 to 4
Outputs:
- scores: float32 [2, 4, 1024], P(None, 'owner', 'cache')
- new_cache: bfloat16 [32, 4, 128, 256], P('cache')
- new_backing: bfloat16 [32, 32, 128, 256], P('cache', 'owner')
Inputs may be any that keep to these rules, and one draw needn't show every extreme that they name: `resident`: for each feature, 4 distinct backing blocks. `promote`: for each feature, 2 distinct backing blocks, none of them in that feature's resident; block k belongs to owner k // 8. `victim`: for each feature, 2 distinct slots. `route`: each batch and owner group holds every request index once.
All inputs are finite; a program needn't handle non-finite values.
Results may differ from a plain program's by a relative error of at most 0.004.
Values may be sent and summed in bfloat16 or wider, within the bound.
A program may use at most 128 MiB of HBM per device.

v0:
```python
import jax
import jax.numpy as jnp
from jax import lax
from jax.sharding import PartitionSpec as P


def take_rows(table, wanted):
    return jax.vmap(lambda rows, chosen: rows[chosen])(table, wanted)


def pool_batch(requests, order, table):
    requests = requests[order]
    count = requests.shape[0]
    step = min(512, count)
    codes = jnp.arange(table.shape[1], dtype=jnp.int32)

    def one_block(lookup_block):
        counts = jnp.sum((lookup_block[..., None] == codes).astype(jnp.bfloat16), axis=2)
        return jnp.einsum("rfk,fke->rfe", counts, table, preferred_element_type=jnp.float32).astype(
            jnp.bfloat16
        )

    blocks = requests.reshape((count // step, step) + requests.shape[1:])
    pooled = lax.map(one_block, blocks)
    return pooled.reshape((count,) + pooled.shape[2:])


def on_device(
    cache,
    backing,
    resident,
    promote,
    victim,
    lookups,
    route,
    dcn_down,
    dcn_up,
    dcn_bias,
    mlp_in,
    mlp_bias,
    mlp_out,
    out_bias,
):
    held = cache.shape[0]
    slots = cache.shape[1]
    block = cache.shape[2]
    width = cache.shape[3]
    own_blocks = backing.shape[1]
    promoted_count = promote.shape[1]
    owner_here = lax.axis_index("owner")
    local_index = promote - owner_here * own_blocks
    owned_here = (local_index >= 0) & (local_index < own_blocks)
    clamped = jnp.clip(local_index, 0, own_blocks - 1)
    fetched = take_rows(backing, clamped)
    outgoing = jnp.where(owned_here[:, :, None, None], fetched, jnp.zeros_like(fetched))
    arrived = lax.all_gather(outgoing, "owner", axis=0, tiled=True)
    owners = arrived.shape[0] // held
    arrived = arrived.reshape(owners, held, promoted_count, block, width)
    source = promote // own_blocks
    picked = source[None] == jnp.arange(owners, dtype=jnp.int32)[:, None, None]
    promoted = jnp.sum(jnp.where(picked[..., None, None], arrived, jnp.zeros_like(arrived)), axis=0)
    evicted = take_rows(cache, victim)
    leaving = take_rows(resident, victim) - owner_here * own_blocks
    slot_numbers = jnp.arange(slots, dtype=jnp.int32)
    block_numbers = jnp.arange(own_blocks, dtype=jnp.int32)
    new_cache = cache
    new_backing = backing
    for column in range(promoted_count):
        slot_hit = victim[:, column][:, None] == slot_numbers[None, :]
        new_cache = jnp.where(slot_hit[:, :, None, None], promoted[:, column][:, None], new_cache)
        block_hit = leaving[:, column][:, None] == block_numbers[None, :]
        new_backing = jnp.where(
            block_hit[:, :, None, None], evicted[:, column][:, None], new_backing
        )
    table = new_cache.reshape(held, slots * block, width)
    batches = lookups.shape[0]
    received = []
    for batch_turn in range(batches):
        pooled = pool_batch(lookups[batch_turn], route[batch_turn, 0], table)
        received.append(lax.all_to_all(pooled, "cache", split_axis=0, concat_axis=1, tiled=True))
    arrived_rows = jnp.stack(received)
    per_batch = arrived_rows.shape[1]
    features = arrived_rows.reshape(batches * per_batch, -1)
    low = jnp.dot(
        features,
        lax.all_gather(dcn_down, "cache", axis=0, tiled=True),
        preferred_element_type=jnp.float32,
    ).astype(jnp.bfloat16)
    gate = (
        jnp.dot(
            low,
            lax.all_gather(dcn_up, "cache", axis=1, tiled=True),
            preferred_element_type=jnp.float32,
        )
        + dcn_bias
    )
    crossed = (features * gate + features).astype(jnp.bfloat16)
    portion = mlp_in.shape[1] // lax.axis_size("owner")
    own_columns = lax.dynamic_slice_in_dim(mlp_in, owner_here * portion, portion, 1)
    column_block = lax.all_gather(own_columns, "cache", axis=0, tiled=True)
    before = jnp.dot(
        crossed,
        lax.all_gather(column_block, "owner", axis=1, tiled=True),
        preferred_element_type=jnp.float32,
    )
    hidden = jnp.maximum(before + mlp_bias, 0.0)
    scores = jnp.sum(hidden * mlp_out, axis=-1) + out_bias[0]
    return (scores.reshape(batches, 1, per_batch), new_cache, new_backing)


def solution(mesh):
    in_specs = (
        P("cache", None, None, None),
        P("cache", "owner", None, None),
        P("cache", None),
        P("cache", None),
        P("cache", None),
        P(None, "owner", "cache", None),
        P(None, "owner", None),
        P("cache", None),
        P(None, "cache"),
        P(),
        P("cache", None),
        P(),
        P(),
        P(),
    )
    out_specs = (
        P(None, "owner", "cache"),
        P("cache", None, None, None),
        P("cache", "owner", None, None),
    )
    return jax.shard_map(
        on_device, mesh=mesh, in_specs=in_specs, out_specs=out_specs, check_vma=False
    )
```

profile of v0, /device:TPU:0, one launch (start us, length us, event | category | flops | bytes accessed | tf_op | source)
XLA Modules:
  0.0 392.6 jit_solution(9065323531690684591)
XLA Ops:
  7.2 1.5 copy-done
  8.8 0.9 constant_dynamic-slice_fusion
  9.7 0.7 fusion.37
  10.4 0.1 copy.112
  10.5 0.1 reshape.223
  10.6 0.7 compare_and_fusion
  11.3 0.1 copy.111
  11.4 2.2 gather_fusion.2
  13.6 0.9 broadcast_select_fusion
  14.5 0.7 all-gather.8.cloned.1.call-update
  15.3 0.5 all-gather.10.cloned.1.call-update
  15.8 70.4 %all-gather.12.cloned.1.call-done = bf16[8192,256]{1,0:T(8,128)(2,1)} async-done(((bf16[1024,256]{1,0:T(8,128)(2,1)}), bf16[8192,256]{1,0:T(8,128)(2,1)}) %all-gather.12.cloned.1.call-update) | async-done | bytes 4194320 | tf_op jit(solution)/shard_map/all_gather | solution.py:100
  86.3 0.6 copy-done.9
  86.9 0.1 copy.110
  87.0 0.2 copy-done.8
  87.2 0.8 copy.137
  88.1 7.9 %gather_fusion = s32[1024,4,8]{2,1,0:T(4,128)} fusion(s32[1024,4,8]{2,1,0:T(4,128)S(1)} %bitcast.100, s32[1024]{0:T(1024)S(1)} %broadcast_clamp_fusion.1), kind=kCustom, calls=%fused_computation | custom fusion | bytes 266240 | tf_op jit(solution)/shard_map/gather | solution.py:12
  96.0 1.8 copy.113
  98.0 10.9 %all-gather.6.cloned.1.call-done = bf16[16,2,128,256]{3,2,1,0:T(8,128)(2,1)} async-done(((bf16[4,2,128,256]{3,2,1,0:T(8,128)(2,1)}), bf16[16,2,128,256]{3,2,1,0:T(8,128)(2,1)}) %all-gather.6.cloned.1.call-update) | async-done | bytes 2097168 | tf_op jit(solution)/shard_map/all_gather | solution.py:56
  108.9 2.1 select_reduce_fusion
  111.1 1.2 select_select_fusion.1
  112.3 1.5 broadcast.130.clone2.1
  113.7 27.7 %while.26 = (s32[]{:T(128)}, bf16[2,512,4,256]{3,1,0,2:T(8,128)(2,1)}, s32[2,512,4,8]{1,3,2,0:T(8,128)S(1)}, bf16[4,512,256]{2,1,0:T(8,128)(2,1)}, s32[]{:T(128)}) while((s32[]{:T(128)}, bf16[2,512,4,256]{3,1,0,2:T(8,128)(2,1)}, s32[2,512,4,8]{1,3,2,0:T(8,128)S(1)}, bf16[4,512,256]{2,1,0:T(8,128)(2,1)}, s32[]{:T(128)}) %tuple.91), condition=%wide.region_3.4_spmd.clone, body=%wide.region_1.3_spmd.clone.sunk | while | flops 561512448 | bytes 10814045 | solution.py:24
  113.8 0.4 copy.164
  114.2 11.7 %fusion.60 = bf16[512,4,512]{2,1,0:T(4,128)(2,1)S(1)} fusion(s32[512,4,8]{2,1,0:T(4,128)S(1)} %copy.164), kind=kLoop, calls=%fused_computation.9.clone.1 | loop fusion | flops 24117248 | bytes 2162688 | tf_op jit(solution)/shard_map/while/body/eval_jaxpr/reduce_sum | solution.py:18
  125.9 1.7 fusion.61
  127.6 0.4 copy.164
  128.0 11.7 %fusion.60 = bf16[512,4,512]{2,1,0:T(4,128)(2,1)S(1)} fusion(s32[512,4,8]{2,1,0:T(4,128)S(1)} %copy.164), kind=kLoop, calls=%fused_computation.9.clone.1 | loop fusion | flops 24117248 | bytes 2162688 | tf_op jit(solution)/shard_map/while/body/eval_jaxpr/reduce_sum | solution.py:18
  139.8 1.7 fusion.61
  141.5 4.5 %copy.115 = bf16[1024,4,256]{2,1,0:T(4,128)(2,1)} copy(bf16[1024,4,256]{2,0,1:T(8,128)(2,1)} %bitcast.12) | data formatting | bytes 4194304 | tf_op jit(solution)/shard_map/reshape | solution.py:25
  146.0 5.5 %all-to-all-start = ((bf16[1024,4,256]{2,1,0:T(4,128)(2,1)}), bf16[1024,4,256]{2,1,0:T(4,128)(2,1)}, u32[]{:S(2)}, u32[]{:S(2)}) async-start(bf16[1024,4,256]{2,1,0:T(4,128)(2,1)} %copy.115), calls=%async_computation | async-start | bytes 4194304 | tf_op jit(solution)/shard_map/all_to_all | solution.py:80
  151.5 0.8 copy.138
  152.3 7.9 %gather_fusion.1 = s32[1024,4,8]{2,1,0:T(4,128)} fusion(s32[1024,4,8]{2,1,0:T(4,128)S(1)} %bitcast.101, s32[1024]{0:T(1024)S(1)} %broadcast_clamp_fusion), kind=kCustom, calls=%fused_computation.1 | custom fusion | bytes 266240 | tf_op jit(solution)/shard_map/gather | solution.py:12
  160.3 1.8 copy.120
  162.1 1.5 broadcast.130.clone2
  163.6 27.7 %while.27 = (s32[]{:T(128)}, bf16[2,512,4,256]{3,1,0,2:T(8,128)(2,1)}, s32[2,512,4,8]{1,3,2,0:T(8,128)S(1)}, bf16[4,512,256]{2,1,0:T(8,128)(2,1)}, s32[]{:T(128)}) while((s32[]{:T(128)}, bf16[2,512,4,256]{3,1,0,2:T(8,128)(2,1)}, s32[2,512,4,8]{1,3,2,0:T(8,128)S(1)}, bf16[4,512,256]{2,1,0:T(8,128)(2,1)}, s32[]{:T(128)}) %tuple.92), condition=%wide.region_6.7_spmd.clone, body=%wide.region_4.6_spmd.clone.sunk | while | flops 561512448 | bytes 10814045 | solution.py:24
  163.6 0.4 copy.166
  164.0 11.7 %fusion.64 = bf16[512,4,512]{2,1,0:T(4,128)(2,1)S(1)} fusion(s32[512,4,8]{2,1,0:T(4,128)S(1)} %copy.166), kind=kLoop, calls=%fused_computation.18.clone.1 | loop fusion | flops 24117248 | bytes 2162688 | tf_op jit(solution)/shard_map/while/body/eval_jaxpr/reduce_sum | solution.py:18
  175.7 1.7 fusion.65
  177.4 0.4 copy.166
  177.9 11.7 %fusion.64 = bf16[512,4,512]{2,1,0:T(4,128)(2,1)S(1)} fusion(s32[512,4,8]{2,1,0:T(4,128)S(1)} %copy.166), kind=kLoop, calls=%fused_computation.18.clone.1 | loop fusion | flops 24117248 | bytes 2162688 | tf_op jit(solution)/shard_map/while/body/eval_jaxpr/reduce_sum | solution.py:18
  189.6 1.7 fusion.65
  191.3 4.6 %copy.122 = bf16[1024,4,256]{2,1,0:T(4,128)(2,1)} copy(bf16[1024,4,256]{2,0,1:T(8,128)(2,1)} %bitcast.20) | data formatting | bytes 4194304 | tf_op jit(solution)/shard_map/reshape | solution.py:25
  195.9 17.7 %all-to-all-done = bf16[1024,4,256]{2,1,0:T(4,128)(2,1)} async-done(((bf16[1024,4,256]{2,1,0:T(4,128)(2,1)}), bf16[1024,4,256]{2,1,0:T(4,128)(2,1)}, u32[]{:S(2)}, u32[]{:S(2)}) %all-to-all-start) | async-done | bytes 2097184 | tf_op jit(solution)/shard_map/all_to_all | solution.py:80
  213.6 4.6 %all-to-all-start.1 = ((bf16[1024,4,256]{2,1,0:T(4,128)(2,1)}), bf16[1024,4,256]{2,1,0:T(4,128)(2,1)}, u32[]{:S(2)}, u32[]{:S(2)}) async-start(bf16[1024,4,256]{2,1,0:T(4,128)(2,1)} %copy.122), calls=%async_computation.1 | async-start | bytes 4194304 | tf_op jit(solution)/shard_map/all_to_all | solution.py:80
  218.9 0.1 copy.126
  219.0 0.1 reshape.229
  219.0 0.6 gather_fusion.4
  219.6 0.7 gather_fusion.3
  220.4 0.2 slice_reduce_fusion.1
  220.7 3.3 select_select_fusion
  224.0 1.9 copy.116
  225.8 1.6 copy.117
  227.4 53.9 %all-to-all-done.1 = bf16[1024,4,256]{2,1,0:T(4,128)(2,1)} async-done(((bf16[1024,4,256]{2,1,0:T(4,128)(2,1)}), bf16[1024,4,256]{2,1,0:T(4,128)(2,1)}, u32[]{:S(2)}, u32[]{:S(2)}) %all-to-all-start.1) | async-done | bytes 2097184 | tf_op jit(solution)/shard_map/all_to_all | solution.py:80
  281.3 1.9 copy.123
  283.2 0.1 copy.124
  283.4 1.5 copy-done.3
  284.9 0.4 pad_maximum_fusion
  285.3 2.4 copy.125
  287.7 6.3 %copy.142 = bf16[32,8,32,256]{3,1,2,0:T(8,128)(2,1)} copy(bf16[32,8,32,256]{3,2,1,0:T(8,128)(2,1)S(1)} %bitcast.99) | data formatting | bytes 8388608
  294.0 4.3 %convolution_convert_fusion = bf16[256,128]{1,0:T(8,128)(2,1)S(1)} fusion(bf16[256,8192]{1,0:T(8,128)(2,1)} %bitcast.97, bf16[8192,128]{1,0:T(8,128)(2,1)} %all-gather.8.cloned.1.call-done), kind=kOutput, calls=%fused_computation.35 | convolution fusion | flops 536903680 | bytes 6356992 | tf_op jit(solution)/shard_map/dot_general | solution.py:84
  298.3 74.4 %all-gather.14.cloned.1.call-done = bf16[8192,1024]{1,0:T(8,128)(2,1)} async-done(((bf16[8192,256]{1,0:T(8,128)(2,1)}), bf16[8192,1024]{1,0:T(8,128)(2,1)}) %all-gather.14.cloned.1.call-update) | async-done | bytes 16777232 | tf_op jit(solution)/shard_map/all_gather | solution.py:103
  372.7 12.8 %fusion.33 = f32[256]{0:T(256)S(1)} fusion(bf16[8192,1024]{1,0:T(8,128)(2,1)} %all-gather.14.cloned.1.call-done, bf16[256,128]{1,0:T(8,128)(2,1)S(1)} %convolution_convert_fusion, bf16[128,8192]{1,0:T(8,128)(2,1)} %all-gather.10.cloned.1.call-done, bf16[256,8192]{1,0:T(8,128)(2,1)} %bitcast.98, f32[8192]{0:T(1024)S(1)} %copy-done.12, ...), kind=kOutput, calls=%fused_computation.34 | convolution fusion | flops 4843372544 | bytes 23176192 | tf_op jit(solution)/shard_map/dot_general | solution.py:101
  385.5 0.6 broadcast_add_fusion
  (58 shorter events, 0.8 us)
Async XLA Ops:
  7.2 1.6 copy-start
  7.2 79.0 %all-gather.12.cloned.1.call-start = ((), (), s32[]{:S(2)}) async-start(), calls=%async_computation.5 | async-start | bytes 4718592 | tf_op jit(solution)/shard_map/all_gather | solution.py:100
  9.6 99.3 %all-gather.6.cloned.1.call-start = ((), (), s32[]{:S(2)}) async-start(), calls=%async_computation.2 | async-start | bytes 2621440 | tf_op jit(solution)/shard_map/all_gather | solution.py:56
  14.5 279.5 %all-gather.8.cloned.1.call-start = ((), (), s32[]{:S(2)}) async-start(), calls=%async_computation.3 | async-start | bytes 2359296 | tf_op jit(solution)/shard_map/all_gather | solution.py:86
  15.2 283.1 %all-gather.10.cloned.1.call-start = ((), (), s32[]{:S(2)}) async-start(), calls=%async_computation.4 | async-start | bytes 2359296 | tf_op jit(solution)/shard_map/all_gather | solution.py:92
  15.8 356.9 %all-gather.14.cloned.1.call-start = ((), (), s32[]{:S(2)}) async-start(), calls=%async_computation.6 | async-start | bytes 20971520 | tf_op jit(solution)/shard_map/all_gather | solution.py:103
  86.2 0.7 copy-start.9
  86.2 1.0 copy-start.8
  86.3 1.8 copy-start.10
  96.0 1.9 copy-start.11
  97.9 13.2 %copy-start.4 = (bf16[4,4,128,256]{3,2,1,0:T(8,128)(2,1)S(1)}, bf16[4,4,128,256]{3,2,1,0:T(8,128)(2,1)}, u32[]{:S(2)}) copy-start(bf16[4,4,128,256]{3,2,1,0:T(8,128)(2,1)} %param.18) | copy-start | bytes 3145732
  114.2 11.7 %copy-start.6 = (bf16[4,512,256]{2,1,0:T(8,128)(2,1)S(1)}, bf16[4,512,256]{2,1,0:T(8,128)(2,1)}, u32[]{:S(2)}) copy-start(bf16[4,512,256]{2,1,0:T(8,128)(2,1)} %get-tuple-element.305) | copy-start | bytes 3145732 | tf_op jit(solution)/shard_map/while
  128.0 11.7 %copy-start.6 = (bf16[4,512,256]{2,1,0:T(8,128)(2,1)S(1)}, bf16[4,512,256]{2,1,0:T(8,128)(2,1)}, u32[]{:S(2)}) copy-start(bf16[4,512,256]{2,1,0:T(8,128)(2,1)} %get-tuple-element.305) | copy-start | bytes 3145732 | tf_op jit(solution)/shard_map/while
  146.0 67.6 %all-to-all-start = ((bf16[1024,4,256]{2,1,0:T(4,128)(2,1)}), bf16[1024,4,256]{2,1,0:T(4,128)(2,1)}, u32[]{:S(2)}, u32[]{:S(2)}) async-start(bf16[1024,4,256]{2,1,0:T(4,128)(2,1)} %copy.115), calls=%async_computation | async-start | bytes 4194304 | tf_op jit(solution)/shard_map/all_to_all | solution.py:80
  164.0 11.7 %copy-start.7 = (bf16[4,512,256]{2,1,0:T(8,128)(2,1)S(1)}, bf16[4,512,256]{2,1,0:T(8,128)(2,1)}, u32[]{:S(2)}) copy-start(bf16[4,512,256]{2,1,0:T(8,128)(2,1)} %get-tuple-element.290) | copy-start | bytes 3145732 | tf_op jit(solution)/shard_map/while
  177.8 11.7 %copy-start.7 = (bf16[4,512,256]{2,1,0:T(8,128)(2,1)S(1)}, bf16[4,512,256]{2,1,0:T(8,128)(2,1)}, u32[]{:S(2)}) copy-start(bf16[4,512,256]{2,1,0:T(8,128)(2,1)} %get-tuple-element.290) | copy-start | bytes 3145732 | tf_op jit(solution)/shard_map/while
  195.9 23.1 %copy-start.5 = (bf16[4,4,128,256]{3,2,1,0:T(8,128)(2,1)S(1)}, bf16[4,4,128,256]{3,2,1,0:T(8,128)(2,1)}, u32[]{:S(2)}) copy-start(bf16[4,4,128,256]{3,2,1,0:T(8,128)(2,1)} %param.18) | copy-start | bytes 3145732
  195.9 23.7 %copy-start.2 = (s32[4,4]{1,0:T(4,128)S(1)}, s32[4,4]{1,0:T(4,128)}, u32[]{:S(2)}) copy-start(s32[4,4]{1,0:T(4,128)} %param.20) | copy-start | bytes 196
  213.6 67.7 %all-to-all-start.1 = ((bf16[1024,4,256]{2,1,0:T(4,128)(2,1)}), bf16[1024,4,256]{2,1,0:T(4,128)(2,1)}, u32[]{:S(2)}, u32[]{:S(2)}) async-start(bf16[1024,4,256]{2,1,0:T(4,128)(2,1)} %copy.122), calls=%async_computation.1 | async-start | bytes 4194304 | tf_op jit(solution)/shard_map/all_to_all | solution.py:80
  283.2 1.6 copy-start.3
  294.0 78.7 %copy-start.12 = (f32[8192]{0:T(1024)S(1)}, f32[8192]{0:T(1024)}, u32[]{:S(2)}) copy-start(f32[8192]{0:T(1024)} %param.27) | copy-start | bytes 98308
  294.0 78.7 %copy-start.13 = (f32[1024]{0:T(1024)S(1)}, f32[1024]{0:T(1024)}, u32[]{:S(2)}) copy-start(f32[1024]{0:T(1024)} %param.30) | copy-start | bytes 12292
  294.0 78.7 %copy-start.14 = (f32[1024]{0:T(1024)S(1)}, f32[1024]{0:T(1024)}, u32[]{:S(2)}) copy-start(f32[1024]{0:T(1024)} %param.29) | copy-start | bytes 12292
  372.7 13.3 %copy-start.1 = (bf16[1024,1024]{1,0:T(8,128)(2,1)S(1)}, bf16[1024,1024]{1,0:T(8,128)(2,1)}, u32[]{:S(2)}) copy-start(bf16[1024,1024]{1,0:T(8,128)(2,1)} %param.28) | copy-start | bytes 6291460
Sparse Core Ops, SparseCore 0:
  10.7 75.4 all-gather.11
  87.8 21.0 all-gather.5
  111.1 52.2 all-gather.7
  165.3 89.3 all-gather.9
  256.1 116.5 all-gather.13
where the time goes:
time: 393 us
  waiting for transfers between devices  229 us (58%)
  local copies, waits for them, and re-layouts  58.2 us (15%)
  other arithmetic  56.9 us (14%)
  matrix products  23.8 us (6%)
  between operations  14.7 us (4%)
  starting transfers between devices  10.3 us (3%)
    all_gather x1, waiting for transfers between devices, on_device(): lax.all_gather(column_block, 'owner', axis=1, tiled=True)  74.4 us
    all_to_all x2, waiting for transfers between devices, on_device(): lax.all_to_all(pooled, 'cache', split_axis=0, concat_axis=1, tiled=True)  71.6 us
    all_gather x1, waiting for transfers between devices, on_device(): column_block = lax.all_gather(own_columns, 'cache', axis=0, tiled=True)  70.4 us
    reduce_sum x4, other arithmetic, one_block(): jnp.sum((lookup_block[..., None] == codes).astype(jnp.bfloat16), axis=2)  46.9 us
    gather x2, local copies, waits for them, and re-layouts, pool_batch(): requests = requests[order]  15.9 us
    unnamed x31, local copies, waits for them, and re-layouts  15.5 us
    dot_general x1, matrix products, on_device(): jnp.dot(crossed, lax.all_gather(column_block, 'owner', axis=1, tiled=True...  12.8 us
    all_gather x1, waiting for transfers between devices, on_device(): arrived = lax.all_gather(outgoing, 'owner', axis=0, tiled=True)  10.9 us
  transfers between devices with their start and end apart: 7, of which 5 were waited for; matrix products, arithmetic and copies ran while one was open for 31% of the time, Pallas kernels for 0%

commit v1 on v0

--- a/solution.py
+++ b/solution.py
@@ -98,10 +98,11 @@
     portion = mlp_in.shape[1] // lax.axis_size("owner")
     own_columns = lax.dynamic_slice_in_dim(mlp_in, owner_here * portion, portion, 1)
     column_block = lax.all_gather(own_columns, "cache", axis=0, tiled=True)
+    save_the_strips_all = lambda panel, dim_k: jnp.concatenate(
+        lax.all_gather(panel, "owner"), dim_k
+    )
     before = jnp.dot(
-        crossed,
-        lax.all_gather(column_block, "owner", axis=1, tiled=True),
-        preferred_element_type=jnp.float32,
+        crossed, save_the_strips_all(column_block, 1), preferred_element_type=jnp.float32
     )
     hidden = jnp.maximum(before + mlp_bias, 0.0)
     scores = jnp.sum(hidden * mlp_out, axis=-1) + out_bias[0]

time: 393 us -> 352 us (0.90)
  waiting for transfers between devices: 229 us -> 164 us
  local copies, waits for them, and re-layouts: 58.2 us -> 85.4 us
  matrix products: 23.8 us -> 19.7 us
    all_gather x1, waiting for transfers between devices: 74.4 us -> 5 us  [on_device(): lax.all_gather(panel, 'owner')]
    all_gather x1, waiting for transfers between devices: 0.02 us -> 29.4 us  [on_device(): lax.all_gather(dcn_up, 'cache', axis=1, tiled=True)]
    all_to_all x2, waiting for transfers between devices: 71.6 us -> 46.4 us  [on_device(): lax.all_to_all(pooled, 'cache', split_axis=0, concat_axis=1, tiled=True)]
    reshape x0 -> x1, local copies, waits for them, and re-layouts: none -> 21.7 us  [on_device(): jnp.concatenate(lax.all_gather(panel, 'owner'), dim_k)]
    while x8 -> x24, local copies, waits for them, and re-layouts: 0.03 us -> 5.31 us
  transfers between devices with their start and end apart: 7 -> 7, of which waited for: 5 -> 6; matrix products, arithmetic and copies ran while one was open for 31% -> 40% of each run, Pallas kernels for 0% -> 0%
where the time goes in v1:
time: 352 us; the launch traced here: 351 us
  waiting for transfers between devices  164 us (47%)
  local copies, waits for them, and re-layouts  85.4 us (24%)
  other arithmetic  57 us (16%)
  matrix products  19.7 us (6%)
  between operations  14.7 us (4%)
  starting transfers between devices  10.3 us (3%)
    all_gather x1, waiting for transfers between devices, on_device(): column_block = lax.all_gather(own_columns, 'cache', axis=0, tiled=True)  70.9 us
    reduce_sum x4, other arithmetic, one_block(): jnp.sum((lookup_block[..., None] == codes).astype(jnp.bfloat16), axis=2)  46.9 us
    all_to_all x2, waiting for transfers between devices, on_device(): lax.all_to_all(pooled, 'cache', split_axis=0, concat_axis=1, tiled=True)  46.4 us
    all_gather x1, waiting for transfers between devices, on_device(): lax.all_gather(dcn_up, 'cache', axis=1, tiled=True)  29.4 us
    reshape x1, local copies, waits for them, and re-layouts, on_device(): jnp.concatenate(lax.all_gather(panel, 'owner'), dim_k)  21.7 us
    gather x2, local copies, waits for them, and re-layouts, pool_batch(): requests = requests[order]  15.9 us
    unnamed x31, local copies, waits for them, and re-layouts  15.6 us
    dot_general x1, matrix products, on_device(): jnp.dot(crossed, save_the_strips_all(column_block, 1), preferred_element_...  12.7 us
  transfers between devices with their start and end apart: 7, of which 6 were waited for; matrix products, arithmetic and copies ran while one was open for 40% of the time, Pallas kernels for 0%

profile of v1, /device:TPU:0, one launch (start us, length us, event | category | flops | bytes accessed | tf_op | source)
XLA Modules:
  0.0 350.8 jit_solution(13821655663095036658)
XLA Ops:
  7.2 1.5 copy-done
  8.8 0.9 constant_dynamic-slice_fusion
  9.7 0.7 fusion.37
  10.6 0.7 compare_and_fusion
  11.4 2.2 gather_fusion.2
  13.6 1.0 broadcast_select_fusion
  14.6 0.7 all-gather.9.cloned.1.call-update
  15.4 70.9 %all-gather.13.cloned.1.call-done = bf16[8192,256]{1,0:T(8,128)(2,1)} async-done(((bf16[1024,256]{1,0:T(8,128)(2,1)}), bf16[8192,256]{1,0:T(8,128)(2,1)}) %all-gather.13.cloned.1.call-update) | async-done | bytes 4194320 | tf_op jit(solution)/shard_map/all_gather | solution.py:100
  86.3 0.9 copy-done.12
  87.2 0.8 copy.142
  88.1 7.9 %gather_fusion.1 = s32[1024,4,8]{2,1,0:T(4,128)} fusion(s32[1024,4,8]{2,1,0:T(4,128)S(1)} %bitcast.106, s32[1024]{0:T(1024)S(1)} %broadcast_clamp_fusion), kind=kCustom, calls=%fused_computation.1 | custom fusion | bytes 266240 | tf_op jit(solution)/shard_map/gather | solution.py:12
  96.0 1.9 copy.123
  98.1 10.8 %all-gather.7.cloned.1.call-done = bf16[16,2,128,256]{3,2,1,0:T(8,128)(2,1)} async-done(((bf16[4,2,128,256]{3,2,1,0:T(8,128)(2,1)}), bf16[16,2,128,256]{3,2,1,0:T(8,128)(2,1)}) %all-gather.7.cloned.1.call-update) | async-done | bytes 2097168 | tf_op jit(solution)/shard_map/all_gather | solution.py:56
  108.9 2.1 select_reduce_fusion
  111.1 1.2 select_select_fusion.1
  112.3 1.5 broadcast.130.clone2
  113.7 28.5 %while.27 = (s32[]{:T(128)}, bf16[2,512,4,256]{3,1,0,2:T(8,128)(2,1)}, s32[2,512,4,8]{1,3,2,0:T(8,128)S(1)}, bf16[4,512,256]{2,1,0:T(8,128)(2,1)}, s32[]{:T(128)}) while((s32[]{:T(128)}, bf16[2,512,4,256]{3,1,0,2:T(8,128)(2,1)}, s32[2,512,4,8]{1,3,2,0:T(8,128)S(1)}, bf16[4,512,256]{2,1,0:T(8,128)(2,1)}, s32[]{:T(128)}) %tuple.91), condition=%wide.region_6.7_spmd.clone, body=%wide.region_4.6_spmd.clone.sunk | while | flops 561512448 | bytes 27590816 | solution.py:24
  113.8 0.4 copy.170
  114.2 11.7 %fusion.64 = bf16[512,4,512]{2,1,0:T(4,128)(2,1)S(1)} fusion(s32[512,4,8]{2,1,0:T(4,128)S(1)} %copy.170), kind=kLoop, calls=%fused_computation.18.clone.1 | loop fusion | flops 24117248 | bytes 2162688 | tf_op jit(solution)/shard_map/while/body/eval_jaxpr/reduce_sum | solution.py:18
  125.9 0.7 fusion.65
  126.7 1.3 copy-done.6
  128.0 0.4 copy.170
  128.4 11.7 %fusion.64 = bf16[512,4,512]{2,1,0:T(4,128)(2,1)S(1)} fusion(s32[512,4,8]{2,1,0:T(4,128)S(1)} %copy.170), kind=kLoop, calls=%fused_computation.18.clone.1 | loop fusion | flops 24117248 | bytes 2162688 | tf_op jit(solution)/shard_map/while/body/eval_jaxpr/reduce_sum | solution.py:18
  140.2 0.7 fusion.65
  140.9 1.3 copy-done.6
  142.2 4.6 %copy.125 = bf16[1024,4,256]{2,1,0:T(4,128)(2,1)} copy(bf16[1024,4,256]{2,0,1:T(8,128)(2,1)} %bitcast.111) | data formatting | bytes 4194304 | tf_op jit(solution)/shard_map/reshape | solution.py:25
  146.8 5.5 %all-to-all-start.1 = ((bf16[1024,4,256]{2,1,0:T(4,128)(2,1)}), bf16[1024,4,256]{2,1,0:T(4,128)(2,1)}, u32[]{:S(2)}, u32[]{:S(2)}) async-start(bf16[1024,4,256]{2,1,0:T(4,128)(2,1)} %copy.125), calls=%async_computation.1 | async-start | bytes 4194304 | tf_op jit(solution)/shard_map/all_to_all | solution.py:80
  152.3 0.8 copy.141
  153.2 7.9 %gather_fusion = s32[1024,4,8]{2,1,0:T(4,128)} fusion(s32[1024,4,8]{2,1,0:T(4,128)S(1)} %bitcast.107, s32[1024]{0:T(1024)S(1)} %broadcast_clamp_fusion.1), kind=kCustom, calls=%fused_computation | custom fusion | bytes 266240 | tf_op jit(solution)/shard_map/gather | solution.py:12
  161.1 1.8 copy.116
  162.9 1.5 broadcast.130.clone2.1
  164.4 28.5 %while.26 = (s32[]{:T(128)}, bf16[2,512,4,256]{3,1,0,2:T(8,128)(2,1)}, s32[2,512,4,8]{1,3,2,0:T(8,128)S(1)}, bf16[4,512,256]{2,1,0:T(8,128)(2,1)}, s32[]{:T(128)}) while((s32[]{:T(128)}, bf16[2,512,4,256]{3,1,0,2:T(8,128)(2,1)}, s32[2,512,4,8]{1,3,2,0:T(8,128)S(1)}, bf16[4,512,256]{2,1,0:T(8,128)(2,1)}, s32[]{:T(128)}) %tuple.92), condition=%wide.region_3.4_spmd.clone, body=%wide.region_1.3_spmd.clone.sunk | while | flops 561512448 | bytes 27590816 | solution.py:24
  164.4 0.4 copy.168
  164.8 11.7 %fusion.60 = bf16[512,4,512]{2,1,0:T(4,128)(2,1)S(1)} fusion(s32[512,4,8]{2,1,0:T(4,128)S(1)} %copy.168), kind=kLoop, calls=%fused_computation.9.clone.1 | loop fusion | flops 24117248 | bytes 2162688 | tf_op jit(solution)/shard_map/while/body/eval_jaxpr/reduce_sum | solution.py:18
  176.6 0.7 fusion.61
  177.3 1.3 copy-done.4
  178.6 0.4 copy.168
  179.1 11.7 %fusion.60 = bf16[512,4,512]{2,1,0:T(4,128)(2,1)S(1)} fusion(s32[512,4,8]{2,1,0:T(4,128)S(1)} %copy.168), kind=kLoop, calls=%fused_computation.9.clone.1 | loop fusion | flops 24117248 | bytes 2162688 | tf_op jit(solution)/shard_map/while/body/eval_jaxpr/reduce_sum | solution.py:18
  190.8 0.7 fusion.61
  191.5 1.3 copy-done.4
  192.9 4.6 %copy.118 = bf16[1024,4,256]{2,1,0:T(4,128)(2,1)} copy(bf16[1024,4,256]{2,0,1:T(8,128)(2,1)} %bitcast.110) | data formatting | bytes 4194304 | tf_op jit(solution)/shard_map/reshape | solution.py:25
  197.5 7.6 %all-to-all-done.1 = bf16[1024,4,256]{2,1,0:T(4,128)(2,1)} async-done(((bf16[1024,4,256]{2,1,0:T(4,128)(2,1)}), bf16[1024,4,256]{2,1,0:T(4,128)(2,1)}, u32[]{:S(2)}, u32[]{:S(2)}) %all-to-all-start.1) | async-done | bytes 2097184 | tf_op jit(solution)/shard_map/all_to_all | solution.py:80
  205.1 4.4 %all-to-all-start = ((bf16[1024,4,256]{2,1,0:T(4,128)(2,1)}), bf16[1024,4,256]{2,1,0:T(4,128)(2,1)}, u32[]{:S(2)}, u32[]{:S(2)}) async-start(bf16[1024,4,256]{2,1,0:T(4,128)(2,1)} %copy.118), calls=%async_computation | async-start | bytes 4194304 | tf_op jit(solution)/shard_map/all_to_all | solution.py:80
  209.5 0.3 all-gather.11.cloned.1.call-start
  209.8 0.3 all-gather.11.cloned.1.call-update
  210.9 0.6 gather_fusion.4
  211.5 0.7 gather_fusion.3
  212.3 0.2 slice_reduce_fusion.1
  212.6 3.2 select_select_fusion
  215.9 1.9 copy.126
  217.7 1.6 copy.127
  219.3 38.8 %all-to-all-done = bf16[1024,4,256]{2,1,0:T(4,128)(2,1)} async-done(((bf16[1024,4,256]{2,1,0:T(4,128)(2,1)}), bf16[1024,4,256]{2,1,0:T(4,128)(2,1)}, u32[]{:S(2)}, u32[]{:S(2)}) %all-to-all-start) | async-done | bytes 2097184 | tf_op jit(solution)/shard_map/all_to_all | solution.py:80
  258.1 1.9 copy.119
  260.0 0.1 copy.120
  260.2 1.4 copy-done.7
  261.6 0.4 pad_maximum_fusion
  262.0 2.4 copy.128
  264.4 6.3 %copy.146 = bf16[32,8,32,256]{3,1,2,0:T(8,128)(2,1)} copy(bf16[32,8,32,256]{3,2,1,0:T(8,128)(2,1)S(1)} %bitcast.105) | data formatting | bytes 8388608
  270.8 4.1 %convolution_convert_fusion = bf16[256,128]{1,0:T(8,128)(2,1)S(1)} fusion(bf16[256,8192]{1,0:T(8,128)(2,1)} %bitcast.103, bf16[8192,128]{1,0:T(8,128)(2,1)} %all-gather.9.cloned.1.call-done), kind=kOutput, calls=%fused_computation.35 | convolution fusion | flops 536903680 | bytes 6356992 | tf_op jit(solution)/shard_map/dot_general | solution.py:84
  274.9 5.0 %all-gather.15.cloned.1.call-done = bf16[32768,256]{1,0:T(8,128)(2,1)} async-done(((bf16[8192,256]{1,0:T(8,128)(2,1)}), bf16[32768,256]{1,0:T(8,128)(2,1)}) %all-gather.15.cloned.1.call-update) | async-done | bytes 16777232 | tf_op jit(solution)/shard_map/all_gather | solution.py:102
  279.9 21.7 %copy.129 = bf16[8192,4,256]{0,2,1:T(8,128)(2,1)} copy(bf16[8192,4,256]{2,0,1:T(8,128)(2,1)} %bitcast.101) | data formatting | bytes 33554432 | tf_op jit(solution)/shard_map/reshape | solution.py:101
  301.6 29.4 %all-gather.11.cloned.1.call-done = bf16[128,8192]{1,0:T(8,128)(2,1)} async-done(((bf16[128,1024]{1,0:T(8,128)(2,1)}), bf16[128,8192]{1,0:T(8,128)(2,1)}) %all-gather.11.cloned.1.call-update) | async-done | bytes 2097168 | tf_op jit(solution)/shard_map/all_gather | solution.py:92
  331.0 12.7 %fusion.33 = f32[256]{0:T(256)S(1)} fusion(bf16[8192,1024]{0,1:T(8,128)(2,1)} %bitcast.102, bf16[256,128]{1,0:T(8,128)(2,1)S(1)} %convolution_convert_fusion, bf16[128,8192]{1,0:T(8,128)(2,1)} %all-gather.11.cloned.1.call-done, bf16[256,8192]{1,0:T(8,128)(2,1)} %bitcast.104, f32[8192]{0:T(1024)S(1)} %copy-done.16, f32[1024]{0:T(1024)S(1)} %copy-done.17, ...), kind=kOutput, calls=%fused_computation.34 | convolution fusion | flops 4843372544 | bytes 23176192 | tf_op jit(solution)/shard_map/dot_general | solution.py:104
  343.7 0.6 broadcast_add_fusion
  (75 shorter events, 1.3 us)
Async XLA Ops:
  7.2 1.6 copy-start
  7.2 79.0 %all-gather.13.cloned.1.call-start = ((), (), s32[]{:S(2)}) async-start(), calls=%async_computation.5 | async-start | bytes 4718592 | tf_op jit(solution)/shard_map/all_gather | solution.py:100
  9.6 99.3 %all-gather.7.cloned.1.call-start = ((), (), s32[]{:S(2)}) async-start(), calls=%async_computation.2 | async-start | bytes 2621440 | tf_op jit(solution)/shard_map/all_gather | solution.py:56
  14.6 256.2 %all-gather.9.cloned.1.call-start = ((), (), s32[]{:S(2)}) async-start(), calls=%async_computation.3 | async-start | bytes 2359296 | tf_op jit(solution)/shard_map/all_gather | solution.py:86
  15.3 264.6 %all-gather.15.cloned.1.call-start = ((), (), s32[]{:S(2)}) async-start(), calls=%async_computation.6 | async-start | bytes 20971520 | tf_op jit(solution)/shard_map/all_gather | solution.py:102
  86.2 0.9 copy-start.12
  86.3 1.8 copy-start.14
  96.0 1.9 copy-start.13
  96.0 2.0 copy-start.15
  97.9 13.2 %copy-start.8 = (bf16[4,4,128,256]{3,2,1,0:T(8,128)(2,1)S(1)}, bf16[4,4,128,256]{3,2,1,0:T(8,128)(2,1)}, u32[]{:S(2)}) copy-start(bf16[4,4,128,256]{3,2,1,0:T(8,128)(2,1)} %param.18) | copy-start | bytes 3145732
  114.2 11.8 %copy-start.5 = (bf16[2,512,4,256]{3,1,0,2:T(8,128)(2,1)S(1)}, bf16[2,512,4,256]{3,1,0,2:T(8,128)(2,1)}, u32[]{:S(2)}) copy-start(bf16[2,512,4,256]{3,1,0,2:T(8,128)(2,1)} %get-tuple-element.283) | copy-start | bytes 6291460 | tf_op jit(solution)/shard_map/while
  114.2 11.8 %copy-start.10 = (bf16[4,512,256]{2,1,0:T(8,128)(2,1)S(1)}, bf16[4,512,256]{2,1,0:T(8,128)(2,1)}, u32[]{:S(2)}) copy-start(bf16[4,512,256]{2,1,0:T(8,128)(2,1)} %get-tuple-element.290) | copy-start | bytes 3145732 | tf_op jit(solution)/shard_map/while
  126.7 1.3 copy-start.6
  128.4 11.8 %copy-start.5 = (bf16[2,512,4,256]{3,1,0,2:T(8,128)(2,1)S(1)}, bf16[2,512,4,256]{3,1,0,2:T(8,128)(2,1)}, u32[]{:S(2)}) copy-start(bf16[2,512,4,256]{3,1,0,2:T(8,128)(2,1)} %get-tuple-element.283) | copy-start | bytes 6291460 | tf_op jit(solution)/shard_map/while
  128.4 11.8 %copy-start.10 = (bf16[4,512,256]{2,1,0:T(8,128)(2,1)S(1)}, bf16[4,512,256]{2,1,0:T(8,128)(2,1)}, u32[]{:S(2)}) copy-start(bf16[4,512,256]{2,1,0:T(8,128)(2,1)} %get-tuple-element.290) | copy-start | bytes 3145732 | tf_op jit(solution)/shard_map/while
  140.9 1.3 copy-start.6
  146.8 58.3 %all-to-all-start.1 = ((bf16[1024,4,256]{2,1,0:T(4,128)(2,1)}), bf16[1024,4,256]{2,1,0:T(4,128)(2,1)}, u32[]{:S(2)}, u32[]{:S(2)}) async-start(bf16[1024,4,256]{2,1,0:T(4,128)(2,1)} %copy.125), calls=%async_computation.1 | async-start | bytes 4194304 | tf_op jit(solution)/shard_map/all_to_all | solution.py:80
  164.8 11.8 %copy-start.3 = (bf16[2,512,4,256]{3,1,0,2:T(8,128)(2,1)S(1)}, bf16[2,512,4,256]{3,1,0,2:T(8,128)(2,1)}, u32[]{:S(2)}) copy-start(bf16[2,512,4,256]{3,1,0,2:T(8,128)(2,1)} %get-tuple-element.298) | copy-start | bytes 6291460 | tf_op jit(solution)/shard_map/while
  164.8 11.8 %copy-start.11 = (bf16[4,512,256]{2,1,0:T(8,128)(2,1)S(1)}, bf16[4,512,256]{2,1,0:T(8,128)(2,1)}, u32[]{:S(2)}) copy-start(bf16[4,512,256]{2,1,0:T(8,128)(2,1)} %get-tuple-element.305) | copy-start | bytes 3145732 | tf_op jit(solution)/shard_map/while
  177.3 1.3 copy-start.4
  179.0 11.8 %copy-start.3 = (bf16[2,512,4,256]{3,1,0,2:T(8,128)(2,1)S(1)}, bf16[2,512,4,256]{3,1,0,2:T(8,128)(2,1)}, u32[]{:S(2)}) copy-start(bf16[2,512,4,256]{3,1,0,2:T(8,128)(2,1)} %get-tuple-element.298) | copy-start | bytes 6291460 | tf_op jit(solution)/shard_map/while
  179.0 11.8 %copy-start.11 = (bf16[4,512,256]{2,1,0:T(8,128)(2,1)S(1)}, bf16[4,512,256]{2,1,0:T(8,128)(2,1)}, u32[]{:S(2)}) copy-start(bf16[4,512,256]{2,1,0:T(8,128)(2,1)} %get-tuple-element.305) | copy-start | bytes 3145732 | tf_op jit(solution)/shard_map/while
  191.5 1.3 copy-start.4
  197.5 13.4 %copy-start.9 = (bf16[4,4,128,256]{3,2,1,0:T(8,128)(2,1)S(1)}, bf16[4,4,128,256]{3,2,1,0:T(8,128)(2,1)}, u32[]{:S(2)}) copy-start(bf16[4,4,128,256]{3,2,1,0:T(8,128)(2,1)} %param.18) | copy-start | bytes 3145732
  197.5 14.0 %copy-start.2 = (s32[4,4]{1,0:T(4,128)S(1)}, s32[4,4]{1,0:T(4,128)}, u32[]{:S(2)}) copy-start(s32[4,4]{1,0:T(4,128)} %param.20) | copy-start | bytes 196
  205.1 53.0 %all-to-all-start = ((bf16[1024,4,256]{2,1,0:T(4,128)(2,1)}), bf16[1024,4,256]{2,1,0:T(4,128)(2,1)}, u32[]{:S(2)}, u32[]{:S(2)}) async-start(bf16[1024,4,256]{2,1,0:T(4,128)(2,1)} %copy.118), calls=%async_computation | async-start | bytes 4194304 | tf_op jit(solution)/shard_map/all_to_all | solution.py:80
  209.5 121.5 %all-gather.11.cloned.1.call-start = ((), (), s32[]{:S(2)}) async-start(), calls=%async_computation.4 | async-start | bytes 2359296 | tf_op jit(solution)/shard_map/all_gather | solution.py:92
  260.0 1.6 copy-start.7
  279.9 51.1 %copy-start.16 = (f32[8192]{0:T(1024)S(1)}, f32[8192]{0:T(1024)}, u32[]{:S(2)}) copy-start(f32[8192]{0:T(1024)} %param.27) | copy-start | bytes 98308
  279.9 51.1 %copy-start.17 = (f32[1024]{0:T(1024)S(1)}, f32[1024]{0:T(1024)}, u32[]{:S(2)}) copy-start(f32[1024]{0:T(1024)} %param.30) | copy-start | bytes 12292
  279.9 51.1 %copy-start.18 = (f32[1024]{0:T(1024)S(1)}, f32[1024]{0:T(1024)}, u32[]{:S(2)}) copy-start(f32[1024]{0:T(1024)} %param.29) | copy-start | bytes 12292
  331.0 13.3 %copy-start.1 = (bf16[1024,1024]{1,0:T(8,128)(2,1)S(1)}, bf16[1024,1024]{1,0:T(8,128)(2,1)}, u32[]{:S(2)}) copy-start(bf16[1024,1024]{1,0:T(8,128)(2,1)} %param.28) | copy-start | bytes 6291460
Sparse Core Ops, SparseCore 0:
  10.7 75.4 all-gather.12
  87.8 21.0 all-gather.6
  111.1 51.5 all-gather.8
  164.1 115.7 all-gather.14
  281.9 49.0 all-gather.10
